TPU v7x, 32 devices: a whole 2x2x4 slice. The times are simulated.
32 devices in a mesh: tile: 8 (over y, x, core), blk: 4 (over z).
Axes of the slice: x: 2, y: 2, z: 4, core: 2. Of those that a mesh axis runs over, the one named last changes fastest.
Arguments:
- model_anoms: bfloat16 [24576, 256], P(('tile', 'blk')), may hold values from -6 to 6
- block_map: int32 [32, 768], P(('tile', 'blk')), may hold values from 0 to 767, each once within a row
- vectors: bfloat16 [2, 24576], P(None, ('tile', 'blk')), may hold values from -6 to 6
- positions: bfloat16 [3, 24576], P(None, ('tile', 'blk')), may hold values from 0 to 3
- pattern: int32 [192, 24], P(('tile', 'blk')), may hold values from 0 to 1, as said below
- pair_scale: float32 [192, 24], P(('tile', 'blk')), may hold values from 0.3 to 1
Outputs:
- applied: float32 [2, 24576], P(None, ('tile', 'blk'))
Inputs may be any that keep to these rules, and one draw needn't show every extreme that they name: pattern is 1 on each block with itself and symmetric within a group of 24 blocks.
All inputs are finite; a program needn't handle non-finite values.
Results may differ from a plain program's by a relative error of at most 0.0003.
Values may be sent and summed in bfloat16 or wider, within the bound.
A program may use at most 64 MiB of HBM per device.

v0:
```python
import jax
import jax.numpy as jnp
from jax import lax
from jax.sharding import PartitionSpec as P

M = 256
BLOCK = 128


def passed_along(value, axis, steps):
    count = lax.axis_size(axis)
    pairs = [(source, (source + steps) % count) for source in range(count)]
    return lax.ppermute(value, axis, pairs)


def gaspari_cohn(own_pos, other_pos):
    dx = own_pos[0][:, None] - other_pos[0][None, :]
    dy = own_pos[1][:, None] - other_pos[1][None, :]
    dz = own_pos[2][:, None] - other_pos[2][None, :]
    dist = jnp.sqrt(dx * dx + dy * dy + dz * dz)
    inner = (((-0.25 * dist + 0.5) * dist + 0.625) * dist - 5.0 / 3.0) * dist * dist + 1.0
    outer = (
        ((((dist / 12.0 - 0.5) * dist + 0.625) * dist + 5.0 / 3.0) * dist - 5.0) * dist
        + 4.0
        - 2.0 / (3.0 * jnp.maximum(dist, 1.0))
    )
    return jnp.where(dist <= 1.0, inner, jnp.where(dist <= 2.0, outer, 0.0))


def on_device(model_anoms, block_map, vectors, positions, pattern, pair_scale):
    received = lax.all_to_all(model_anoms, "tile", split_axis=0, concat_axis=0, tiled=True)
    anoms = jnp.take(received, block_map[0], axis=0)
    rows = anoms.shape[0]
    blocks_here = rows // BLOCK
    links = pattern.astype(jnp.float32) * pair_scale
    own_pos = positions.astype(jnp.float32)
    cycle_size = lax.axis_size("blk")
    place = lax.axis_index("blk")

    def contribution(panel, source):
        part_anoms, part_pos, part_vecs = panel
        cov = lax.dot_general(
            anoms, part_anoms, (((1,), (1,)), ((), ())), preferred_element_type=jnp.float32
        )
        kern = gaspari_cohn(own_pos, part_pos.astype(jnp.float32))
        weight = lax.dynamic_slice_in_dim(links, source * blocks_here, blocks_here, 1)
        taper = (
            (cov * kern).reshape(blocks_here, BLOCK, blocks_here, BLOCK) * weight[:, None, :, None]
        ).reshape(rows, rows) / (M - 1)
        return lax.dot_general(
            part_vecs.astype(jnp.float32),
            taper,
            (((1,), (1,)), ((), ())),
            precision=lax.Precision.HIGHEST,
        )

    def forward(panel):
        return passed_along((panel[0], panel[1], panel[2]), "blk", 1)

    panel = (anoms, positions, vectors)
    total = contribution(panel, place)

    def one_step(step, carry):
        ahead, summed = carry
        ahead = forward(ahead)
        summed = summed + contribution(ahead, (place - step) % cycle_size)
        return (ahead, summed)

    ahead, total = lax.fori_loop(1, cycle_size, one_step, (panel, total))
    return total


def solution(mesh):
    return jax.shard_map(
        on_device,
        mesh=mesh,
        in_specs=(
            P(("tile", "blk"), None),
            P(("tile", "blk"), None),
            P(None, ("tile", "blk")),
            P(None, ("tile", "blk")),
            P(("tile", "blk"), None),
            P(("tile", "blk"), None),
        ),
        out_specs=P(None, ("tile", "blk")),
        check_vma=False,
    )
```

profile of v0, /device:TPU:2, one launch (start us, length us, event | category | flops | bytes accessed | tf_op | source)
XLA Modules:
  0.0 75.8 jit_solution(17930007563023860207)
XLA Ops:
  0.0 0.7 copy.38
  0.7 0.7 copy.39
  1.4 4.3 %all-to-all-start = ((bf16[8,96,256]{2,1,0:T(8,128)(2,1)}), bf16[8,96,256]{2,1,0:T(8,128)(2,1)S(1)}, u32[]{:S(2)}, u32[]{:S(2)}) async-start(bf16[8,96,256]{2,1,0:T(8,128)(2,1)} %bitcast.47), calls=%async_computation | async-start | bytes 786432 | tf_op jit(solution)/shard_map/all_to_all | solution.py:31
  5.6 0.7 fusion.77
  6.3 0.7 convert_multiply_fusion
  7.1 0.1 constant_dynamic-slice_fusion.1
  7.1 0.7 reduce.6
  7.9 4.6 %all-to-all-done = bf16[8,96,256]{2,1,0:T(8,128)(2,1)S(1)} async-done(((bf16[8,96,256]{2,1,0:T(8,128)(2,1)}), bf16[8,96,256]{2,1,0:T(8,128)(2,1)S(1)}, u32[]{:S(2)}, u32[]{:S(2)}) %all-to-all-start) | async-done | bytes 393248 | tf_op jit(solution)/shard_map/all_to_all | solution.py:31
  12.5 2.6 %gather_fusion = bf16[768,256]{1,0:T(8,128)(2,1)S(1)} fusion(bf16[768,256]{1,0:T(8,128)(2,1)S(1)} %bitcast.45, s32[1024]{0:T(1024)S(1)} %pad_clamp_fusion), kind=kCustom, calls=%fused_computation | custom fusion | bytes 789504 | tf_op jit(solution)/shard_map/jit(_take)/gather | solution.py:32
  15.1 0.2 broadcast_select_fusion
  15.3 0.5 fusion.93
  15.8 0.3 mul.249
  16.1 4.8 %fusion.74 = f32[2,768]{1,0:T(2,128)S(1)} fusion(bf16[2,768]{1,0:T(2,128)(2,1)S(1)} %copy.38, f32[768,768]{1,0:T(8,128)S(1)} %fusion.93, f32[96,8,6,128]{3,2,1,0:T(8,128)S(1)} %bitcast.46, f32[768]{0:T(1024)S(1)} %get-tuple-element.237, f32[768]{0:T(1024)S(1)} %get-tuple-element.238, f32[768]{0:T(1024)S(1)} %get-tuple-element.236), kind=kOutput, calls=%fused_computation.80 | convolution fusion | flops 36569088 | bytes 4737024 | tf_op jit(solution)/shard_map/dot_general | solution.py:50
  20.9 54.2 %while.21 = (s32[]{:T(128)}, bf16[768,256]{1,0:T(8,128)(2,1)S(1)}, bf16[3,768]{1,0:T(4,128)(2,1)S(1)}, bf16[2,768]{1,0:T(2,128)(2,1)S(1)}, f32[2,768]{1,0:T(2,12...) while((s32[]{:T(128)}, bf16[768,256]{1,0:T(8,128)(2,1)S(1)}, ...), condition=%wide.region_1.2_spmd, body=%wide.region_0.1_spmd.sunk | while | flops 338562816 | bytes 12714336 | solution.py:69
  21.0 1.6 %collective-permute-start = (bf16[768,256]{1,0:T(8,128)(2,1)S(1)}, bf16[768,256]{1,0:T(8,128)(2,1)S(1)}, u32[]{:S(2)}, u32[]{:S(2)}) collective-permute-start(bf16[768,256]{1,0:T(8,128)(2,1)S(1)} %get-tuple-element.340), channel_id=1, source_target_pairs={{0,1},{1,2},{2,3},{3,0},{4,5},{5,6},{6,7},{7,4},{8,9},{9,10},{10,1... | collective-permute-start | bytes 1179656 | tf_op jit(solution)/shard_map/while/body/eval_jaxpr/ppermute | solution.py:13
  22.7 1.6 %collective-permute-start.2 = (bf16[2,768]{1,0:T(2,128)(2,1)S(1)}, bf16[2,768]{1,0:T(2,128)(2,1)S(1)}, u32[]{:S(2)}, u32[]{:S(2)}) collective-permute-start(bf16[2,768]{1,0:T(2,128)(2,1)S(1)} %get-tuple-element.342), channel_id=1, source_target_pairs={{0,1},{1,2},{2,3},{3,0},{4,5},{5,6},{6,7},{7,4},{8,9},{9,10},{10,1... | collective-permute-start | bytes 9224 | tf_op jit(solution)/shard_map/while/body/eval_jaxpr/ppermute | solution.py:13
  24.2 1.6 %collective-permute-start.1 = (bf16[3,768]{1,0:T(4,128)(2,1)S(1)}, bf16[3,768]{1,0:T(4,128)(2,1)S(1)}, u32[]{:S(2)}, u32[]{:S(2)}) collective-permute-start(bf16[3,768]{1,0:T(4,128)(2,1)S(1)} %get-tuple-element.341), channel_id=1, source_target_pairs={{0,1},{1,2},{2,3},{3,0},{4,5},{5,6},{6,7},{7,4},{8,9},{9,10},{10,1... | collective-permute-start | bytes 13832 | tf_op jit(solution)/shard_map/while/body/eval_jaxpr/ppermute | solution.py:13
  25.9 0.1 constant_dynamic-slice_fusion.3
  25.9 8.2 %collective-permute-done.2 = bf16[2,768]{1,0:T(2,128)(2,1)S(1)} collective-permute-done((bf16[2,768]{1,0:T(2,128)(2,1)S(1)}, bf16[2,768]{1,0:T(2,128)(2,1)S(1)}, u32[]{:S(2)}, u32[]{:S(2)}) %collective-permute-start.2) | collective-permute-done | bytes 3104 | tf_op jit(solution)/shard_map/while/body/eval_jaxpr/ppermute | solution.py:13
  34.2 0.1 collective-permute-done.1
  34.3 0.0 collective-permute-done
  34.3 0.5 fusion.110
  34.8 0.3 mul.500
  35.1 4.8 %fusion.111 = f32[2,768]{1,0:T(2,128)S(1)} fusion(f32[2,768]{1,0:T(2,128)S(1)} %get-tuple-element.343, bf16[2,768]{1,0:T(2,128)(2,1)S(1)} %collective-permute-done.2, f32[768,768]{1,0:T(8,128)S(1)} %fusion.110, f32[96,8,6,128]{3,2,1,0:T(8,128)S(1)} %bitcast.44, f32[768]{0:T(1024)S(1)} %get-tuple-element.318, f32[768]{0:T(1024)S(1)} %get-tuple-element.319, ...), kind=kOutput, calls=%fused_computation.30.clone.1 | convolution fusion | flops 36570624 | bytes 4752384 | tf_op jit(solution)/shard_map/while/body/eval_jaxpr/dot_general | solution.py:50
  39.9 0.1 collective-permute-start
  40.0 1.3 %collective-permute-start.2 = (bf16[2,768]{1,0:T(2,128)(2,1)S(1)}, bf16[2,768]{1,0:T(2,128)(2,1)S(1)}, u32[]{:S(2)}, u32[]{:S(2)}) collective-permute-start(bf16[2,768]{1,0:T(2,128)(2,1)S(1)} %get-tuple-element.342), channel_id=1, source_target_pairs={{0,1},{1,2},{2,3},{3,0},{4,5},{5,6},{6,7},{7,4},{8,9},{9,10},{10,1... | collective-permute-start | bytes 9224 | tf_op jit(solution)/shard_map/while/body/eval_jaxpr/ppermute | solution.py:13
  41.3 1.6 %collective-permute-start.1 = (bf16[3,768]{1,0:T(4,128)(2,1)S(1)}, bf16[3,768]{1,0:T(4,128)(2,1)S(1)}, u32[]{:S(2)}, u32[]{:S(2)}) collective-permute-start(bf16[3,768]{1,0:T(4,128)(2,1)S(1)} %get-tuple-element.341), channel_id=1, source_target_pairs={{0,1},{1,2},{2,3},{3,0},{4,5},{5,6},{6,7},{7,4},{8,9},{9,10},{10,1... | collective-permute-start | bytes 13832 | tf_op jit(solution)/shard_map/while/body/eval_jaxpr/ppermute | solution.py:13
  42.9 0.1 constant_dynamic-slice_fusion.3
  43.0 9.2 %collective-permute-done.2 = bf16[2,768]{1,0:T(2,128)(2,1)S(1)} collective-permute-done((bf16[2,768]{1,0:T(2,128)(2,1)S(1)}, bf16[2,768]{1,0:T(2,128)(2,1)S(1)}, u32[]{:S(2)}, u32[]{:S(2)}) %collective-permute-start.2) | collective-permute-done | bytes 3104 | tf_op jit(solution)/shard_map/while/body/eval_jaxpr/ppermute | solution.py:13
  52.2 0.1 collective-permute-done.1
  52.3 0.0 collective-permute-done
  52.4 0.5 fusion.110
  52.9 0.3 mul.500
  53.2 4.8 %fusion.111 = f32[2,768]{1,0:T(2,128)S(1)} fusion(f32[2,768]{1,0:T(2,128)S(1)} %get-tuple-element.343, bf16[2,768]{1,0:T(2,128)(2,1)S(1)} %collective-permute-done.2, f32[768,768]{1,0:T(8,128)S(1)} %fusion.110, f32[96,8,6,128]{3,2,1,0:T(8,128)S(1)} %bitcast.44, f32[768]{0:T(1024)S(1)} %get-tuple-element.318, f32[768]{0:T(1024)S(1)} %get-tuple-element.319, ...), kind=kOutput, calls=%fused_computation.30.clone.1 | convolution fusion | flops 36570624 | bytes 4752384 | tf_op jit(solution)/shard_map/while/body/eval_jaxpr/dot_general | solution.py:50
  58.0 0.1 collective-permute-start
  58.0 0.1 collective-permute-start.2
  58.1 0.9 %collective-permute-start.1 = (bf16[3,768]{1,0:T(4,128)(2,1)S(1)}, bf16[3,768]{1,0:T(4,128)(2,1)S(1)}, u32[]{:S(2)}, u32[]{:S(2)}) collective-permute-start(bf16[3,768]{1,0:T(4,128)(2,1)S(1)} %get-tuple-element.341), channel_id=1, source_target_pairs={{0,1},{1,2},{2,3},{3,0},{4,5},{5,6},{6,7},{7,4},{8,9},{9,10},{10,1... | collective-permute-start | bytes 13832 | tf_op jit(solution)/shard_map/while/body/eval_jaxpr/ppermute | solution.py:13
  59.1 0.1 constant_dynamic-slice_fusion.3
  59.1 10.2 %collective-permute-done.2 = bf16[2,768]{1,0:T(2,128)(2,1)S(1)} collective-permute-done((bf16[2,768]{1,0:T(2,128)(2,1)S(1)}, bf16[2,768]{1,0:T(2,128)(2,1)S(1)}, u32[]{:S(2)}, u32[]{:S(2)}) %collective-permute-start.2) | collective-permute-done | bytes 3104 | tf_op jit(solution)/shard_map/while/body/eval_jaxpr/ppermute | solution.py:13
  69.4 0.1 collective-permute-done.1
  69.5 0.0 collective-permute-done
  69.6 0.5 fusion.110
  70.1 0.3 mul.500
  70.3 4.8 %fusion.111 = f32[2,768]{1,0:T(2,128)S(1)} fusion(f32[2,768]{1,0:T(2,128)S(1)} %get-tuple-element.343, bf16[2,768]{1,0:T(2,128)(2,1)S(1)} %collective-permute-done.2, f32[768,768]{1,0:T(8,128)S(1)} %fusion.110, f32[96,8,6,128]{3,2,1,0:T(8,128)S(1)} %bitcast.44, f32[768]{0:T(1024)S(1)} %get-tuple-element.318, f32[768]{0:T(1024)S(1)} %get-tuple-element.319, ...), kind=kOutput, calls=%fused_computation.30.clone.1 | convolution fusion | flops 36570624 | bytes 4752384 | tf_op jit(solution)/shard_map/while/body/eval_jaxpr/dot_general | solution.py:50
  75.2 0.0 copy-start
  75.2 0.6 copy-done
  (23 shorter events, 0.4 us)
Async XLA Ops:
  1.4 11.1 %all-to-all-start = ((bf16[8,96,256]{2,1,0:T(8,128)(2,1)}), bf16[8,96,256]{2,1,0:T(8,128)(2,1)S(1)}, u32[]{:S(2)}, u32[]{:S(2)}) async-start(bf16[8,96,256]{2,1,0:T(8,128)(2,1)} %bitcast.47), calls=%async_computation | async-start | bytes 786432 | tf_op jit(solution)/shard_map/all_to_all | solution.py:31
  21.0 13.3 %collective-permute-start = (bf16[768,256]{1,0:T(8,128)(2,1)S(1)}, bf16[768,256]{1,0:T(8,128)(2,1)S(1)}, u32[]{:S(2)}, u32[]{:S(2)}) collective-permute-start(bf16[768,256]{1,0:T(8,128)(2,1)S(1)} %get-tuple-element.340), channel_id=1, source_target_pairs={{0,1},{1,2},{2,3},{3,0},{4,5},{5,6},{6,7},{7,4},{8,9},{9,10},{10,1... | collective-permute-start | bytes 1179656 | tf_op jit(solution)/shard_map/while/body/eval_jaxpr/ppermute | solution.py:13
  22.7 11.5 %collective-permute-start.2 = (bf16[2,768]{1,0:T(2,128)(2,1)S(1)}, bf16[2,768]{1,0:T(2,128)(2,1)S(1)}, u32[]{:S(2)}, u32[]{:S(2)}) collective-permute-start(bf16[2,768]{1,0:T(2,128)(2,1)S(1)} %get-tuple-element.342), channel_id=1, source_target_pairs={{0,1},{1,2},{2,3},{3,0},{4,5},{5,6},{6,7},{7,4},{8,9},{9,10},{10,1... | collective-permute-start | bytes 9224 | tf_op jit(solution)/shard_map/while/body/eval_jaxpr/ppermute | solution.py:13
  24.2 10.0 %collective-permute-start.1 = (bf16[3,768]{1,0:T(4,128)(2,1)S(1)}, bf16[3,768]{1,0:T(4,128)(2,1)S(1)}, u32[]{:S(2)}, u32[]{:S(2)}) collective-permute-start(bf16[3,768]{1,0:T(4,128)(2,1)S(1)} %get-tuple-element.341), channel_id=1, source_target_pairs={{0,1},{1,2},{2,3},{3,0},{4,5},{5,6},{6,7},{7,4},{8,9},{9,10},{10,1... | collective-permute-start | bytes 13832 | tf_op jit(solution)/shard_map/while/body/eval_jaxpr/ppermute | solution.py:13
  39.9 12.4 %collective-permute-start = (bf16[768,256]{1,0:T(8,128)(2,1)S(1)}, bf16[768,256]{1,0:T(8,128)(2,1)S(1)}, u32[]{:S(2)}, u32[]{:S(2)}) collective-permute-start(bf16[768,256]{1,0:T(8,128)(2,1)S(1)} %get-tuple-element.340), channel_id=1, source_target_pairs={{0,1},{1,2},{2,3},{3,0},{4,5},{5,6},{6,7},{7,4},{8,9},{9,10},{10,1... | collective-permute-start | bytes 1179656 | tf_op jit(solution)/shard_map/while/body/eval_jaxpr/ppermute | solution.py:13
  40.0 12.2 %collective-permute-start.2 = (bf16[2,768]{1,0:T(2,128)(2,1)S(1)}, bf16[2,768]{1,0:T(2,128)(2,1)S(1)}, u32[]{:S(2)}, u32[]{:S(2)}) collective-permute-start(bf16[2,768]{1,0:T(2,128)(2,1)S(1)} %get-tuple-element.342), channel_id=1, source_target_pairs={{0,1},{1,2},{2,3},{3,0},{4,5},{5,6},{6,7},{7,4},{8,9},{9,10},{10,1... | collective-permute-start | bytes 9224 | tf_op jit(solution)/shard_map/while/body/eval_jaxpr/ppermute | solution.py:13
  41.3 11.0 %collective-permute-start.1 = (bf16[3,768]{1,0:T(4,128)(2,1)S(1)}, bf16[3,768]{1,0:T(4,128)(2,1)S(1)}, u32[]{:S(2)}, u32[]{:S(2)}) collective-permute-start(bf16[3,768]{1,0:T(4,128)(2,1)S(1)} %get-tuple-element.341), channel_id=1, source_target_pairs={{0,1},{1,2},{2,3},{3,0},{4,5},{5,6},{6,7},{7,4},{8,9},{9,10},{10,1... | collective-permute-start | bytes 13832 | tf_op jit(solution)/shard_map/while/body/eval_jaxpr/ppermute | solution.py:13
  58.0 11.5 %collective-permute-start = (bf16[768,256]{1,0:T(8,128)(2,1)S(1)}, bf16[768,256]{1,0:T(8,128)(2,1)S(1)}, u32[]{:S(2)}, u32[]{:S(2)}) collective-permute-start(bf16[768,256]{1,0:T(8,128)(2,1)S(1)} %get-tuple-element.340), channel_id=1, source_target_pairs={{0,1},{1,2},{2,3},{3,0},{4,5},{5,6},{6,7},{7,4},{8,9},{9,10},{10,1... | collective-permute-start | bytes 1179656 | tf_op jit(solution)/shard_map/while/body/eval_jaxpr/ppermute | solution.py:13
  58.0 11.3 %collective-permute-start.2 = (bf16[2,768]{1,0:T(2,128)(2,1)S(1)}, bf16[2,768]{1,0:T(2,128)(2,1)S(1)}, u32[]{:S(2)}, u32[]{:S(2)}) collective-permute-start(bf16[2,768]{1,0:T(2,128)(2,1)S(1)} %get-tuple-element.342), channel_id=1, source_target_pairs={{0,1},{1,2},{2,3},{3,0},{4,5},{5,6},{6,7},{7,4},{8,9},{9,10},{10,1... | collective-permute-start | bytes 9224 | tf_op jit(solution)/shard_map/while/body/eval_jaxpr/ppermute | solution.py:13
  58.1 11.3 %collective-permute-start.1 = (bf16[3,768]{1,0:T(4,128)(2,1)S(1)}, bf16[3,768]{1,0:T(4,128)(2,1)S(1)}, u32[]{:S(2)}, u32[]{:S(2)}) collective-permute-start(bf16[3,768]{1,0:T(4,128)(2,1)S(1)} %get-tuple-element.341), channel_id=1, source_target_pairs={{0,1},{1,2},{2,3},{3,0},{4,5},{5,6},{6,7},{7,4},{8,9},{9,10},{10,1... | collective-permute-start | bytes 13832 | tf_op jit(solution)/shard_map/while/body/eval_jaxpr/ppermute | solution.py:13
  75.2 0.6 copy-start
where the time goes:
time: 76.2 us; the launch traced here: 75.8 us
  waiting for transfers between devices  32.5 us (43%)
  matrix products  21.3 us (28%)
  starting transfers between devices  13 us (17%)
  local copies, waits for them, and re-layouts  6.36 us (8%)
  other arithmetic  2.31 us (3%)
    ppermute x9, waiting for transfers between devices, passed_along(): return lax.ppermute(value, axis, pairs)  27.9 us
    dot_general x4, matrix products, contribution(): lax.dot_general(part_vecs.astype(jnp.float32), taper, (((1,), (1,)), ((),...  19.3 us
    ppermute x9, starting transfers between devices, passed_along(): return lax.ppermute(value, axis, pairs)  8.74 us
    all_to_all x1, waiting for transfers between devices, on_device(): lax.all_to_all(model_anoms, 'tile', split_axis=0, concat_axis=0, tiled=True)  4.58 us
    all_to_all x1, starting transfers between devices, on_device(): lax.all_to_all(model_anoms, 'tile', split_axis=0, concat_axis=0, tiled=True)  4.25 us
    gather x1, local copies, waits for them, and re-layouts, on_device(): anoms = jnp.take(received, block_map[0], axis=0)  2.65 us
    dot_general x4, matrix products, contribution(): lax.dot_general(anoms, part_anoms, (((1,), (1,)), ((), ())), preferred_el...  2.01 us
    unnamed x5, local copies, waits for them, and re-layouts  2 us
  transfers between devices with their start and end apart: 10, of which 7 were waited for; matrix products, arithmetic and copies ran while one was open for 4% of the time, Pallas kernels for 0%

commit v1 on v0

v1 whole, which is shorter than its diff:
```python
import functools

import jax
import jax.numpy as jnp
from jax import lax
from jax.experimental import pallas as pl
from jax.experimental.pallas import tpu as pltpu
from jax.sharding import PartitionSpec as P

BLOCK = 128
F32, BF16 = jnp.float32, jnp.bfloat16
MESH = pl.DeviceIdType.MESH
NT = (((1,), (1,)), ((), ()))
TN = (((0,), (0,)), ((), ()))
NN = (((1,), (0,)), ((), ()))


def dot(a, b, dims):
    return lax.dot_general(a, b, dims, preferred_element_type=F32)


def parts(x):
    high = x.astype(BF16).astype(F32)
    rest = x - high
    mid = rest.astype(BF16).astype(F32)
    return high, mid, rest - mid


def stacked(rows, width):
    at = lax.broadcasted_iota(jnp.int32, (16, width), 0)
    out = jnp.zeros((16, width), F32)
    for i, row in enumerate(rows):
        out = jnp.where(at == i, row, out)
    return out


def squared_length(x, y, z):
    return x * x + y * y + z * z


def gaspari_cohn(squared):
    squared = jnp.maximum(squared, 1e-20)
    inverse = lax.rsqrt(squared)
    r = squared * inverse
    t = jnp.maximum(2.0 - r, 0.0)
    t = t * t
    outer = (t * t) * (r * (1.0 / 12.0) + (1.0 / 6.0) - inverse * (1.0 / 24.0))
    inner = (((-0.25 * r + 0.5) * r + 0.625) * r - 5.0 / 3.0) * squared + 1.0
    return jnp.where(squared <= 1.0, inner, outer)


def kernel(n, tiles, blocks, exchange, anoms_ref, side_ref, back_ref, own_w_ref, out_ref,
           buf, sides, backs, one_hot, own_hot, own, p_aug, q_aug, v_col, w_row, acc,
           gave, got, a_send, a_recv, z_send, z_recv, s_send, s_recv, g_send, g_recv, local):
    tile, place = lax.axis_index("tile"), lax.axis_index("blk")
    half = n // 2
    pieces, piece, members = buf.shape[1:]
    rows = pieces * piece
    flip = lax.rem(tile, 2)

    def mirrored(i):
        return i + flip * (n - 1 - 2 * i)

    u = mirrored(place)

    barrier = pltpu.get_barrier_semaphore()
    greeted = n - 1
    for k in range(1, n):
        pl.semaphore_signal(barrier, inc=1, device_id=(tile, lax.rem(place + k, n)), device_id_type=MESH)
    if exchange:
        greeted += tiles - 1
        for k in range(1, tiles):
            pl.semaphore_signal(barrier, inc=1, device_id=(lax.rem(tile + k, tiles), place), device_id_type=MESH)
    pl.semaphore_wait(barrier, greeted)

    def exchanged(k):
        peer = lax.rem(tile + k, tiles)
        slot = place + lax.rem(peer, 2) * (n - 1 - 2 * place)
        return pltpu.make_async_remote_copy(
            src_ref=anoms_ref.at[peer], dst_ref=buf.at[slot, tile], send_sem=a_send.at[k],
            recv_sem=a_recv.at[k], device_id=(peer, place), device_id_type=MESH)

    def moved(j, c, to):
        return pltpu.make_async_remote_copy(
            src_ref=buf.at[j, c], dst_ref=buf.at[j, c], send_sem=z_send.at[j, c],
            recv_sem=z_recv.at[j, c], device_id=(tile, mirrored(to)), device_id_type=MESH)

    def side_moved(j, to, which):
        ref = (sides, backs)[which]
        return pltpu.make_async_remote_copy(
            src_ref=ref.at[j], dst_ref=ref.at[j], send_sem=s_send.at[j, which],
            recv_sem=s_recv.at[j, which], device_id=(tile, mirrored(to)), device_id_type=MESH)

    def given(j, source):
        return pltpu.make_async_remote_copy(
            src_ref=gave.at[j], dst_ref=got.at[source], send_sem=g_send.at[j],
            recv_sem=g_recv.at[source], device_id=(tile, mirrored(j)), device_id_type=MESH)

    sends_right = u < half
    sends_left = u > half
    sends_own = u != half
    own_to = jnp.where(u < half, u + 1, jnp.maximum(u - 1, 0))

    if exchange:
        for k in range(1, tiles):
            exchanged(k).start()
        here = [pltpu.make_async_copy(anoms_ref.at[tile], buf.at[u, tile], local.at[0])]
    else:
        here = [pltpu.make_async_copy(anoms_ref, buf.at[u], local.at[0])]
    here.append(pltpu.make_async_copy(side_ref, sides.at[u], local.at[1]))
    here.append(pltpu.make_async_copy(back_ref, backs.at[u], local.at[2]))
    for copy in here:
        copy.start()
    for copy in here:
        copy.wait()

    @pl.when(sends_own)
    def _():
        side_moved(u, own_to, 0).start()
        side_moved(u, own_to, 1).start()

    def piece_at(k):
        return lax.rem(tile + pieces - k, pieces) if exchange else k

    for k in range(pieces):
        if exchange and k > 0:
            exchanged(k).wait_recv()

        @pl.when(sends_own)
        def _():
            moved(u, piece_at(k), own_to).start()

    def hot_of(j, ref):
        row = sides[j, 5:6, :].astype(jnp.int32)
        for c in range(0, rows, BLOCK):
            at = lax.broadcasted_iota(jnp.int32, (BLOCK, rows), 0) + c
            ref[c:c + BLOCK, :] = jnp.where(at == row, 1.0, 0.0).astype(BF16)

    def prepare(j, hot, back):
        side = sides[j]
        w = own_w_ref[mirrored(j)]
        values = list(parts(side[3:4] * w)) + list(parts(side[4:5] * w)) + [side]
        if back:
            table = backs[j, place]
            column = lax.broadcasted_iota(jnp.int32, (8, rows), 1) // BLOCK
            wide = jnp.zeros((8, rows), F32)
            for b in range(blocks):
                wide = jnp.where(column == b, table[:, b:b + 1], wide)
            values += list(parts(wide))
        if len(values) % 2:
            values.append(jnp.zeros((8, rows), F32))
        turned = dot(jnp.concatenate(values, axis=0).astype(BF16), hot[...], NT)
        lines = [turned[0:8] + turned[8:16] + turned[16:24], turned[24:32] + turned[32:40] + turned[40:48]]
        if back:
            lines.append(turned[56:64] + turned[64:72] + turned[72:80])
        for b in range(blocks):
            for i, line in enumerate(lines):
                w_row[b, i:i + 1, :] = line[b:b + 1]
        x, y, z = turned[48:49], turned[49:50], turned[50:51]
        q_aug[...] = stacked(
            [-2.0 * x, -2.0 * y, -2.0 * z, 1.0, 1.0, 1.0, *parts(squared_length(x, y, z))],
            rows).astype(BF16)

    chunk = 2 * BLOCK
    per_chunk = rows // chunk

    def pair(j, back):
        if back:
            gave[j] = jnp.zeros((8, rows), F32)

        def one(b, carry):
            start = pl.multiple_of(b * BLOCK, BLOCK)
            mine = own[pl.ds(start, BLOCK), :]
            mine_aug = p_aug[:, pl.ds(start, BLOCK)]
            theirs = buf[j].reshape(rows, members)
            sums = [jnp.zeros((BLOCK, BLOCK), F32)] * 2
            for c in range(per_chunk):
                cut = slice(c * chunk, (c + 1) * chunk)
                cov = dot(mine, theirs[cut], NT)
                kern = cov * gaspari_cohn(dot(mine_aug, q_aug[:, cut], TN))
                for v in range(2):
                    term = kern * w_row[b, v:v + 1, cut]
                    sums[v] = sums[v] + term[:, :BLOCK] + term[:, BLOCK:]
                    if back:
                        column = v_col[v, pl.ds(start, BLOCK), :]
                        for s in range(2):
                            lanes = slice(c * chunk + s * BLOCK, c * chunk + (s + 1) * BLOCK)
                            down = jnp.sum(kern[:, s * BLOCK:(s + 1) * BLOCK] * column, axis=0, keepdims=True)
                            gave[j, v:v + 1, lanes] += down * w_row[b, 2:3, lanes]
            for v in range(2):
                acc[v, pl.ds(start, BLOCK), :] += sums[v]
            return carry

        lax.fori_loop(0, blocks, one, 0)

    acc[...] = jnp.zeros_like(acc)
    hot_of(u, own_hot)
    own[...] = dot(own_hot[...], buf[u].reshape(rows, members), TN).astype(BF16)
    side = sides[u]
    x, y, z = side[0:1], side[1:2], side[2:3]
    p_aug[...] = stacked(
        [x, y, z, *parts(squared_length(x, y, z)), 1.0, 1.0, 1.0], rows).astype(BF16)
    both = stacked([side[3:4], side[4:5]], rows).astype(BF16)
    for v in range(2):
        pick = jnp.where(lax.broadcasted_iota(jnp.int32, (16, BLOCK), 0) == v, 1.0, 0.0).astype(BF16)
        v_col[v] = dot(both, pick, TN)
    prepare(u, own_hot, False)
    pair(u, False)

    from_left = jnp.minimum(u, half)

    def arrive(j, onward, to):
        side_moved(j, to, 0).wait_recv()
        side_moved(j, to, 1).wait_recv()

        @pl.when(onward)
        def _():
            side_moved(j, to, 0).start()
            side_moved(j, to, 1).start()

        for k in range(pieces):
            moved(j, piece_at(k), to).wait_recv()

            @pl.when(onward)
            def _():
                moved(j, piece_at(k), to).start()

    def work(j):
        hot_of(j, one_hot)
        prepare(j, one_hot, True)
        pair(j, True)
        given(j, u).start()

    def distance(d, carry):
        right = from_left - d
        left = u + d

        @pl.when(right >= 0)
        def _():
            arrive(right, u < n - 1, jnp.minimum(u + 1, n - 1))
            work(right)

        @pl.when((u >= half) & (left < n))
        def _():
            arrive(left, u > half, jnp.maximum(u - 1, 0))
            work(left)

        return carry

    lax.fori_loop(1, max(half, n - 1 - half) + 1, distance, 0)

    total = jnp.zeros((8, rows), F32)
    got_any = []
    for other in range(n):
        comes = ((u < half) & (other > u)) | ((u > half) & (other >= half) & (other < u))

        @pl.when(comes)
        def _():
            given(other, other).wait_recv()

        @pl.when(jnp.logical_not(comes))
        def _():
            got[other] = jnp.zeros((8, rows), F32)

        total = total + got[other]
    returned = jnp.concatenate([*parts(total), jnp.zeros((8, rows), F32)], axis=0).astype(BF16)
    turned = dot(returned, own_hot[...], NN)
    out = turned[0:8] + turned[8:16] + turned[16:24]
    ones = jnp.ones((8, BLOCK), F32)
    for v in range(2):
        line = lax.dot_general(ones, acc[v], NT, precision=lax.Precision.HIGHEST, preferred_element_type=F32)
        out_ref[v:v + 1, :] = out[v:v + 1] + line[0:1]

    if exchange:
        for k in range(1, tiles):
            exchanged(k).wait_send()
    for j in range(n):
        passes = ((j == u) & sends_own) | ((j < from_left) & (u < n - 1)) | ((j > u) & (u > half))

        @pl.when(passes)
        def _():
            side_moved(j, own_to, 0).wait_send()
            side_moved(j, own_to, 1).wait_send()
            for c in range(pieces):
                moved(j, c, own_to).wait_send()

        @pl.when((j < from_left) | ((j > u) & (u >= half)))
        def _():
            given(j, u).wait_send()


def on_device(n, tiles, model_anoms, block_map, vectors, positions, pattern, pair_scale):
    rows, members = model_anoms.shape
    blocks = rows // BLOCK
    exchange = rows % (16 * tiles) == 0
    if exchange:
        pieces = tiles
        anoms = model_anoms.reshape(pieces, rows // pieces, members)
    else:
        pieces = rows // BLOCK
        anoms = lax.all_to_all(model_anoms, "tile", split_axis=0, concat_axis=0, tiled=True)
        anoms = anoms.reshape(pieces, rows // pieces, members)
    side = jnp.concatenate([
        positions.astype(F32), vectors.astype(F32), block_map.astype(F32), jnp.zeros((2, rows), F32)], axis=0)
    links = (pattern.astype(F32) * pair_scale / (members - 1)).reshape(blocks, n, blocks)
    back = jnp.pad(jnp.transpose(links, (1, 2, 0)), ((0, 0), (0, 8 - blocks), (0, BLOCK - blocks)))
    own_w = jnp.pad(jnp.repeat(jnp.transpose(links, (1, 0, 2)), BLOCK, axis=2), ((0, 0), (0, 8 - blocks), (0, 0)))
    vmem = pl.BlockSpec(memory_space=pltpu.VMEM)
    dma = pltpu.SemaphoreType.DMA
    return pl.pallas_call(
        functools.partial(kernel, n, tiles, blocks, exchange),
        out_shape=jax.ShapeDtypeStruct((2, rows), F32),
        in_specs=[vmem] * 4,
        out_specs=vmem,
        scratch_shapes=[
            pltpu.VMEM((n, pieces, rows // pieces, members), BF16),
            pltpu.VMEM((n, 8, rows), F32),
            pltpu.VMEM((n, n, 8, BLOCK), F32),
            pltpu.VMEM((rows, rows), BF16),
            pltpu.VMEM((rows, rows), BF16),
            pltpu.VMEM((rows, members), BF16),
            pltpu.VMEM((16, rows), BF16),
            pltpu.VMEM((16, rows), BF16),
            pltpu.VMEM((2, rows, BLOCK), F32),
            pltpu.VMEM((blocks, 8, rows), F32),
            pltpu.VMEM((2, rows, BLOCK), F32),
            pltpu.VMEM((n, 8, rows), F32),
            pltpu.VMEM((n, 8, rows), F32),
            dma((tiles,)), dma((tiles,)),
            dma((n, pieces)), dma((n, pieces)),
            dma((n, 2)), dma((n, 2)),
            dma((n,)), dma((n,)),
            dma((3,)),
        ],
        compiler_params=pltpu.CompilerParams(
            collective_id=0, has_side_effects=True, vmem_limit_bytes=56 * 2**20),
    )(anoms, side, back, own_w)


def solution(mesh):
    shape = dict(mesh.shape)
    return jax.shard_map(
        functools.partial(on_device, shape["blk"], shape["tile"]),
        mesh=mesh,
        in_specs=(
            P(("tile", "blk"), None),
            P(("tile", "blk"), None),
            P(None, ("tile", "blk")),
            P(None, ("tile", "blk")),
            P(("tile", "blk"), None),
            P(("tile", "blk"), None),
        ),
        out_specs=P(None, ("tile", "blk")),
        check_vma=False,
    )
```

time: 76.2 us -> 49.2 us (0.65)
  the two profiles are of different devices: /device:TPU:2 before, /device:TPU:0 now
where the time goes in v1:
time: 49.2 us; the launch traced here: 48.8 us
  Pallas kernels  43 us (87%)
  local copies, waits for them, and re-layouts  4.39 us (9%)
  other arithmetic  1.4 us (3%)
    pallas_call x1, Pallas kernels, on_device(): pl.pallas_call(functools.partial(kernel, n, tiles, blocks, exchange), out...  43 us
    unnamed x7, local copies, waits for them, and re-layouts  2.73 us

profile of v1, /device:TPU:0, one launch (start us, length us, event | category | flops | bytes accessed | tf_op | source)
XLA Modules:
  0.0 48.8 jit_solution(6889467316790208474)
XLA Ops:
  0.0 0.7 %multiply_multiply_fusion = f32[6,24]{1,0:T(8,128)S(1)} fusion(f32[6,24]{1,0:T(8,128)} %param.11, s32[6,24]{1,0:T(8,128)} %param.10), kind=kLoop, calls=%fused_computation.1 | loop fusion | flops 432 | bytes 1728 | tf_op jit(solution)/shard_map/div | solution.py:305
  0.7 0.1 reshape.10
  0.8 0.1 broadcast_in_dim.7
  0.9 0.6 %pad.9.own_w_ref = f32[4,8,768]{2,1,0:T(8,128)} pad(f32[4,6,768]{2,1,0:T(8,128)S(1)} %copy.10, f32[]{:T(128)} %constant.2.clone.1), padding=0_0x0_2x0_0 | pad | bytes 172036 | tf_op jit(solution)/shard_map/jit(_pad)/pad | solution.py:307
  1.6 0.1 copy.9
  1.7 0.0 copy-start
  1.7 0.6 %pad.8.back_ref = f32[4,8,128]{2,1,0:T(8,128)} pad(f32[4,6,6]{2,1,0:T(8,128)S(1)} %bitcast.7, f32[]{:T(128)} %constant.2.clone.1), padding=0_0x0_2x0_122 | pad | bytes 16964 | tf_op jit(solution)/shard_map/jit(_pad)/pad | solution.py:306
  2.3 0.1 copy-done
  2.4 0.0 copy-start.2
  2.4 0.7 %copy-done.2 = bf16[2,768]{1,0:T(2,128)(2,1)S(1)} copy-done((bf16[2,768]{1,0:T(2,128)(2,1)S(1)}, bf16[2,768]{1,0:T(2,128)(2,1)}, u32[]{:S(2)}) %copy-start.2) | copy-done | bytes 3096
  3.1 0.0 copy-start.1
  3.1 0.7 %copy-done.1 = s32[1,768]{1,0:T(1,128)S(1)} copy-done((s32[1,768]{1,0:T(1,128)S(1)}, s32[1,768]{1,0:T(1,128)}, u32[]{:S(2)}) %copy-start.1) | copy-done | bytes 3096
  3.8 0.1 pad.13.clone
  3.9 0.7 %maximum_maximum_fusion.side_ref = f32[8,768]{1,0:T(8,128)} fusion(f32[1,768]{1,0:T(1,128)S(1)} %convert_element_type.18, f32[2,768]{1,0:T(2,128)S(1)} %convert_element_type.17, f32[3,768]{1,0:T(4,128)S(1)} %convert_element_type.16, f32[8]{0:T(128)S(1)} %pad.13.clone), kind=kLoop, calls=%fused_computation | loop fusion | flops 18432 | bytes 43040 | tf_op jit(solution)/shard_map/concatenate | solution.py:303
  4.5 43.0 %shard_map.64 = f32[2,768]{1,0:T(2,128)} custom-call(bf16[8,96,256]{2,1,0:T(8,128)(2,1)} %bitcast.5, f32[8,768]{1,0:T(8,128)} %maximum_maximum_fusion.side_ref, f32[4,8,128]{2,1,0:T(8,128)} %pad.8.back_ref, f32[4,8,768]{2,1,0:T(8,128)} %pad.9.own_w_ref), custom_call_target="tpu_custom_call" | custom-call | tf_op jit(solution)/shard_map/pallas_call | solution.py:310
  47.5 1.3 %copy.12 = f32[2,768]{1,0:T(2,128)} copy(f32[2,768]{1,0:T(2,128)} %shard_map.64) | data formatting | bytes 12288
  (6 shorter events, 0.1 us)
Async XLA Ops:
  1.7 0.7 %copy-start = (bf16[3,768]{1,0:T(4,128)(2,1)S(1)}, bf16[3,768]{1,0:T(4,128)(2,1)}, u32[]{:S(2)}) copy-start(bf16[3,768]{1,0:T(4,128)(2,1)} %param.9) | copy-start | bytes 13828
  2.4 0.7 %copy-start.2 = (bf16[2,768]{1,0:T(2,128)(2,1)S(1)}, bf16[2,768]{1,0:T(2,128)(2,1)}, u32[]{:S(2)}) copy-start(bf16[2,768]{1,0:T(2,128)(2,1)} %param.8) | copy-start | bytes 9220
  3.1 0.7 %copy-start.1 = (s32[1,768]{1,0:T(1,128)S(1)}, s32[1,768]{1,0:T(1,128)}, u32[]{:S(2)}) copy-start(s32[1,768]{1,0:T(1,128)} %param.7) | copy-start | bytes 9220

commit v2 on v1

--- a/solution.py
+++ b/solution.py
@@ -26,9 +26,9 @@
     return high, mid, rest - mid
 
 
-def stacked(rows, width):
-    at = lax.broadcasted_iota(jnp.int32, (16, width), 0)
-    out = jnp.zeros((16, width), F32)
+def stacked(rows, width, height=16):
+    at = lax.broadcasted_iota(jnp.int32, (height, width), 0)
+    out = jnp.zeros((height, width), F32)
     for i, row in enumerate(rows):
         out = jnp.where(at == i, row, out)
     return out
@@ -49,9 +49,11 @@
     return jnp.where(squared <= 1.0, inner, outer)
 
 
-def kernel(n, tiles, blocks, exchange, anoms_ref, side_ref, back_ref, own_w_ref, out_ref,
-           buf, sides, backs, one_hot, own_hot, own, p_aug, q_aug, v_col, w_row, acc,
-           gave, got, a_send, a_recv, z_send, z_recv, s_send, s_recv, g_send, g_recv, local):
+def kernel(n, tiles, blocks, exchange, anoms_ref, *refs):
+    small_refs, (out_ref, buf), slots = refs[:5], refs[5:7], refs[7:12]
+    (one_hot, own_hot, own, p_aug, q_aug, v_col, w_row, acc,
+     gave, got, a_send, a_recv, z_send, z_recv, s_send, s_recv, g_send, g_recv, local) = refs[12:]
+    positions, vectors, maps, patterns, scales = slots
     tile, place = lax.axis_index("tile"), lax.axis_index("blk")
     half = n // 2
     pieces, piece, members = buf.shape[1:]
@@ -86,7 +88,7 @@
             recv_sem=z_recv.at[j, c], device_id=(tile, mirrored(to)), device_id_type=MESH)
 
     def side_moved(j, to, which):
-        ref = (sides, backs)[which]
+        ref = slots[which]
         return pltpu.make_async_remote_copy(
             src_ref=ref.at[j], dst_ref=ref.at[j], send_sem=s_send.at[j, which],
             recv_sem=s_recv.at[j, which], device_id=(tile, mirrored(to)), device_id_type=MESH)
@@ -107,17 +109,20 @@
         here = [pltpu.make_async_copy(anoms_ref.at[tile], buf.at[u, tile], local.at[0])]
     else:
         here = [pltpu.make_async_copy(anoms_ref, buf.at[u], local.at[0])]
-    here.append(pltpu.make_async_copy(side_ref, sides.at[u], local.at[1]))
-    here.append(pltpu.make_async_copy(back_ref, backs.at[u], local.at[2]))
+    for i in range(5):
+        here.append(pltpu.make_async_copy(small_refs[i], slots[i].at[u], local.at[i + 1]))
     for copy in here:
         copy.start()
     for copy in here:
         copy.wait()
 
-    @pl.when(sends_own)
+    def small_start(j, to):
+        for i in range(5):
+            side_moved(j, to, i).start()
+
+    @pl.when(sends_right)
     def _():
-        side_moved(u, own_to, 0).start()
-        side_moved(u, own_to, 1).start()
+        small_start(u, own_to)
 
     def piece_at(k):
         return lax.rem(tile + pieces - k, pieces) if exchange else k
@@ -126,27 +131,43 @@
         if exchange and k > 0:
             exchanged(k).wait_recv()
 
-        @pl.when(sends_own)
+        @pl.when(sends_right)
         def _():
             moved(u, piece_at(k), own_to).start()
 
     def hot_of(j, ref):
-        row = sides[j, 5:6, :].astype(jnp.int32)
+        row = maps[j]
         for c in range(0, rows, BLOCK):
             at = lax.broadcasted_iota(jnp.int32, (BLOCK, rows), 0) + c
             ref[c:c + BLOCK, :] = jnp.where(at == row, 1.0, 0.0).astype(BF16)
 
+    def link_parts(j):
+        links = patterns[j].astype(F32) * scales[j] / (members - 1)
+        if blocks % 8:
+            links = jnp.concatenate([links, jnp.zeros((8 - blocks, n * blocks), F32)], axis=0)
+        return jnp.concatenate(parts(links), axis=0).astype(BF16)
+
     def prepare(j, hot, back):
-        side = sides[j]
-        w = own_w_ref[mirrored(j)]
-        values = list(parts(side[3:4] * w)) + list(parts(side[4:5] * w)) + [side]
+        where = positions[j].astype(F32)
+        vecs = vectors[j].astype(F32)
+        side = stacked([where[0:1], where[1:2], where[2:3]], rows, 8)
+        columns = n * blocks
+        block_of = lax.broadcasted_iota(jnp.int32, (columns, rows), 1) // BLOCK
+        at = lax.broadcasted_iota(jnp.int32, (columns, rows), 0)
+        spread = jnp.where(at == block_of + mirrored(j) * blocks, 1.0, 0.0).astype(BF16)
+        w = dot(link_parts(u), spread, NN)
+        w = w[0:8] + w[8:16] + w[16:24]
+        values = list(parts(vecs[0:1] * w)) + list(parts(vecs[1:2] * w)) + [side]
         if back:
-            table = backs[j, place]
-            column = lax.broadcasted_iota(jnp.int32, (8, rows), 1) // BLOCK
-            wide = jnp.zeros((8, rows), F32)
-            for b in range(blocks):
-                wide = jnp.where(column == b, table[:, b:b + 1], wide)
-            values += list(parts(wide))
+            take = jnp.where(
+                lax.broadcasted_iota(jnp.int32, (columns, 8), 0)
+                == lax.broadcasted_iota(jnp.int32, (columns, 8), 1) + place * blocks, 1.0, 0.0).astype(BF16)
+            taken = dot(link_parts(j), take, NN)
+            repeated = jnp.where(
+                lax.broadcasted_iota(jnp.int32, (8, rows), 1) // BLOCK
+                == lax.broadcasted_iota(jnp.int32, (8, rows), 0), 1.0, 0.0)
+            for i in range(3):
+                values.append(dot(taken[8 * i:8 * i + 8].astype(BF16), repeated.astype(BF16), TN))
         if len(values) % 2:
             values.append(jnp.zeros((8, rows), F32))
         turned = dot(jnp.concatenate(values, axis=0).astype(BF16), hot[...], NT)
@@ -196,27 +217,33 @@
     acc[...] = jnp.zeros_like(acc)
     hot_of(u, own_hot)
     own[...] = dot(own_hot[...], buf[u].reshape(rows, members), TN).astype(BF16)
-    side = sides[u]
-    x, y, z = side[0:1], side[1:2], side[2:3]
+    where = positions[u].astype(F32)
+    x, y, z = where[0:1], where[1:2], where[2:3]
     p_aug[...] = stacked(
         [x, y, z, *parts(squared_length(x, y, z)), 1.0, 1.0, 1.0], rows).astype(BF16)
-    both = stacked([side[3:4], side[4:5]], rows).astype(BF16)
+    vecs = vectors[u].astype(F32)
+    both = stacked([vecs[0:1], vecs[1:2]], rows).astype(BF16)
     for v in range(2):
         pick = jnp.where(lax.broadcasted_iota(jnp.int32, (16, BLOCK), 0) == v, 1.0, 0.0).astype(BF16)
         v_col[v] = dot(both, pick, TN)
     prepare(u, own_hot, False)
     pair(u, False)
 
+    @pl.when(sends_left)
+    def _():
+        small_start(u, own_to)
+        for k in range(pieces):
+            moved(u, piece_at(k), own_to).start()
+
     from_left = jnp.minimum(u, half)
 
     def arrive(j, onward, to):
-        side_moved(j, to, 0).wait_recv()
-        side_moved(j, to, 1).wait_recv()
+        for i in range(5):
+            side_moved(j, to, i).wait_recv()
 
         @pl.when(onward)
         def _():
-            side_moved(j, to, 0).start()
-            side_moved(j, to, 1).start()
+            small_start(j, to)
 
         for k in range(pieces):
             moved(j, piece_at(k), to).wait_recv()
@@ -231,14 +258,22 @@
         pair(j, True)
         given(j, u).start()
 
+    def arrive_right_going(d):
+        right = from_left - d
+
+        @pl.when(right >= 0)
+        def _():
+            arrive(right, u < n - 1, jnp.minimum(u + 1, n - 1))
+
     def distance(d, carry):
         right = from_left - d
         left = u + d
 
         @pl.when(right >= 0)
         def _():
-            arrive(right, u < n - 1, jnp.minimum(u + 1, n - 1))
             work(right)
+
+        arrive_right_going(d + 1)
 
         @pl.when((u >= half) & (left < n))
         def _():
@@ -247,6 +282,7 @@
 
         return carry
 
+    arrive_right_going(1)
     lax.fori_loop(1, max(half, n - 1 - half) + 1, distance, 0)
 
     total = jnp.zeros((8, rows), F32)
@@ -279,8 +315,8 @@
 
         @pl.when(passes)
         def _():
-            side_moved(j, own_to, 0).wait_send()
-            side_moved(j, own_to, 1).wait_send()
+            for i in range(5):
+                side_moved(j, own_to, i).wait_send()
             for c in range(pieces):
                 moved(j, c, own_to).wait_send()
 
@@ -300,22 +336,20 @@
         pieces = rows // BLOCK
         anoms = lax.all_to_all(model_anoms, "tile", split_axis=0, concat_axis=0, tiled=True)
         anoms = anoms.reshape(pieces, rows // pieces, members)
-    side = jnp.concatenate([
-        positions.astype(F32), vectors.astype(F32), block_map.astype(F32), jnp.zeros((2, rows), F32)], axis=0)
-    links = (pattern.astype(F32) * pair_scale / (members - 1)).reshape(blocks, n, blocks)
-    back = jnp.pad(jnp.transpose(links, (1, 2, 0)), ((0, 0), (0, 8 - blocks), (0, BLOCK - blocks)))
-    own_w = jnp.pad(jnp.repeat(jnp.transpose(links, (1, 0, 2)), BLOCK, axis=2), ((0, 0), (0, 8 - blocks), (0, 0)))
     vmem = pl.BlockSpec(memory_space=pltpu.VMEM)
     dma = pltpu.SemaphoreType.DMA
     return pl.pallas_call(
         functools.partial(kernel, n, tiles, blocks, exchange),
         out_shape=jax.ShapeDtypeStruct((2, rows), F32),
-        in_specs=[vmem] * 4,
+        in_specs=[vmem] * 6,
         out_specs=vmem,
         scratch_shapes=[
             pltpu.VMEM((n, pieces, rows // pieces, members), BF16),
-            pltpu.VMEM((n, 8, rows), F32),
-            pltpu.VMEM((n, n, 8, BLOCK), F32),
+            pltpu.VMEM((n, 3, rows), BF16),
+            pltpu.VMEM((n, 2, rows), BF16),
+            pltpu.VMEM((n, 1, rows), jnp.int32),
+            pltpu.VMEM((n, blocks, n * blocks), jnp.int32),
+            pltpu.VMEM((n, blocks, n * blocks), F32),
             pltpu.VMEM((rows, rows), BF16),
             pltpu.VMEM((rows, rows), BF16),
             pltpu.VMEM((rows, members), BF16),
@@ -328,13 +362,13 @@
             pltpu.VMEM((n, 8, rows), F32),
             dma((tiles,)), dma((tiles,)),
             dma((n, pieces)), dma((n, pieces)),
-            dma((n, 2)), dma((n, 2)),
+            dma((n, 5)), dma((n, 5)),
             dma((n,)), dma((n,)),
-            dma((3,)),
+            dma((6,)),
         ],
         compiler_params=pltpu.CompilerParams(
             collective_id=0, has_side_effects=True, vmem_limit_bytes=56 * 2**20),
-    )(anoms, side, back, own_w)
+    )(anoms, positions, vectors, block_map, pattern, pair_scale)
 
 
 def solution(mesh):

time: 49.2 us -> 40.1 us (0.82)
  Pallas kernels: 43 us -> 38.6 us
  local copies, waits for them, and re-layouts: 4.39 us -> 1.29 us
  other arithmetic: 1.4 us -> 0 us
    pallas_call x1, Pallas kernels: 43 us -> 38.6 us  [on_device(): pl.pallas_call(functools.partial(kernel, n, tiles, blocks, exchange), out...]
    unnamed x7 -> x1, local copies, waits for them, and re-layouts: 2.73 us -> 1.29 us
    pad x2 -> x0, local copies, waits for them, and re-layouts: 1.25 us -> none  [the longest x1 0.64 us: on_device(): jnp.pad(jnp.repeat(jnp.transpose(links, (1, 0, 2)), BLOCK, axis=2), ((0,...]
    div x1 -> x0, other arithmetic: 0.71 us -> none  [on_device(): pattern.astype(F32) * pair_scale / (members - 1)]
    concatenate x1 -> x0, other arithmetic: 0.68 us -> none  [on_device(): jnp.concatenate([positions.astype(F32), vectors.astype(F32), block_map.as...]
where the time goes in v2:
time: 40.1 us; the launch traced here: 39.9 us
  Pallas kernels  38.6 us (96%)
  local copies, waits for them, and re-layouts  1.29 us (3%)
    pallas_call x1, Pallas kernels, on_device(): pl.pallas_call(functools.partial(kernel, n, tiles, blocks, exchange), out...  38.6 us
    unnamed x1, local copies, waits for them, and re-layouts  1.29 us

profile of v2, /device:TPU:0, one launch (start us, length us, event | category | flops | bytes accessed | tf_op | source)
XLA Modules:
  0.0 39.9 jit_solution(12354182661336026300)
XLA Ops:
  0.0 38.6 %shard_map.64 = f32[2,768]{1,0:T(2,128)} custom-call(bf16[8,96,256]{2,1,0:T(8,128)(2,1)} %bitcast.1, bf16[3,768]{1,0:T(4,128)(2,1)} %refs_0_.1, bf16[2,768]{1,0:T(2,128)(2,1)} %refs_1_.1, s32[1,768]{1,0:T(1,128)} %refs_2_.1, s32[6,24]{1,0:T(8,128)} %refs_3_.1, f32[6,24]{1,0:T(8,128)} %refs_4_.1), custom_call_target="tpu_custom_call" | custom-call | tf_op jit(solution)/shard_map/pallas_call | solution.py:341
  38.6 1.3 %copy.8 = f32[2,768]{1,0:T(2,128)} copy(f32[2,768]{1,0:T(2,128)} %shard_map.64) | data formatting | bytes 12288

commit v3 on v2

--- a/solution.py
+++ b/solution.py
@@ -182,14 +182,42 @@
             [-2.0 * x, -2.0 * y, -2.0 * z, 1.0, 1.0, 1.0, *parts(squared_length(x, y, z))],
             rows).astype(BF16)
 
+    from_left = jnp.minimum(u, half)
+
+    def arrive_small(j, onward, to):
+        @pl.when(j >= 0)
+        def _():
+            for i in range(5):
+                side_moved(j, to, i).wait_recv()
+
+            @pl.when(onward)
+            def _():
+                small_start(j, to)
+
+    def arrive_piece(j, c, onward, to):
+        moved(j, c, to).wait_recv()
+
+        @pl.when(onward)
+        def _():
+            moved(j, c, to).start()
+
     chunk = 2 * BLOCK
     per_chunk = rows // chunk
 
-    def pair(j, back):
+    def pair(j, back, following):
         if back:
             gave[j] = jnp.zeros((8, rows), F32)
 
+        onward, to = u < n - 1, jnp.minimum(u + 1, n - 1)
+        arrive_small(following, onward, to)
+
         def one(b, carry):
+            first, last = lax.div(b * pieces, blocks), lax.div((b + 1) * pieces, blocks)
+            for i in range(-(-pieces // blocks)):
+                @pl.when((following >= 0) & (first + i < last))
+                def _():
+                    arrive_piece(following, piece_at(first + i), onward, to)
+
             start = pl.multiple_of(b * BLOCK, BLOCK)
             mine = own[pl.ds(start, BLOCK), :]
             mine_aug = p_aug[:, pl.ds(start, BLOCK)]
@@ -227,7 +255,7 @@
         pick = jnp.where(lax.broadcasted_iota(jnp.int32, (16, BLOCK), 0) == v, 1.0, 0.0).astype(BF16)
         v_col[v] = dot(both, pick, TN)
     prepare(u, own_hot, False)
-    pair(u, False)
+    pair(u, False, from_left - 1)
 
     @pl.when(sends_left)
     def _():
@@ -235,35 +263,11 @@
         for k in range(pieces):
             moved(u, piece_at(k), own_to).start()
 
-    from_left = jnp.minimum(u, half)
-
-    def arrive(j, onward, to):
-        for i in range(5):
-            side_moved(j, to, i).wait_recv()
-
-        @pl.when(onward)
-        def _():
-            small_start(j, to)
-
-        for k in range(pieces):
-            moved(j, piece_at(k), to).wait_recv()
-
-            @pl.when(onward)
-            def _():
-                moved(j, piece_at(k), to).start()
-
-    def work(j):
+    def work(j, following):
         hot_of(j, one_hot)
         prepare(j, one_hot, True)
-        pair(j, True)
+        pair(j, True, following)
         given(j, u).start()
-
-    def arrive_right_going(d):
-        right = from_left - d
-
-        @pl.when(right >= 0)
-        def _():
-            arrive(right, u < n - 1, jnp.minimum(u + 1, n - 1))
 
     def distance(d, carry):
         right = from_left - d
@@ -271,18 +275,18 @@
 
         @pl.when(right >= 0)
         def _():
-            work(right)
-
-        arrive_right_going(d + 1)
+            work(right, right - 1)
 
         @pl.when((u >= half) & (left < n))
         def _():
-            arrive(left, u > half, jnp.maximum(u - 1, 0))
-            work(left)
+            onward, to = u > half, jnp.maximum(u - 1, 0)
+            arrive_small(left, onward, to)
+            for k in range(pieces):
+                arrive_piece(left, piece_at(k), onward, to)
+            work(left, -1)
 
         return carry
 
-    arrive_right_going(1)
     lax.fori_loop(1, max(half, n - 1 - half) + 1, distance, 0)
 
     total = jnp.zeros((8, rows), F32)

time: 40.1 us -> 43.5 us (1.085)
  Pallas kernels: 38.6 us -> 42 us
    pallas_call x1, Pallas kernels: 38.6 us -> 42 us  [on_device(): pl.pallas_call(functools.partial(kernel, n, tiles, blocks, exchange), out...]
where the time goes in v3:
time: 43.5 us; the launch traced here: 43.3 us
  Pallas kernels  42 us (97%)
  local copies, waits for them, and re-layouts  1.29 us (3%)
    pallas_call x1, Pallas kernels, on_device(): pl.pallas_call(functools.partial(kernel, n, tiles, blocks, exchange), out...  42 us
    unnamed x1, local copies, waits for them, and re-layouts  1.29 us

profile of v3, /device:TPU:0, one launch (start us, length us, event | category | flops | bytes accessed | tf_op | source)
XLA Modules:
  0.0 43.3 jit_solution(3652678060337781988)
XLA Ops:
  0.0 42.0 %shard_map.64 = f32[2,768]{1,0:T(2,128)} custom-call(bf16[8,96,256]{2,1,0:T(8,128)(2,1)} %bitcast.1, bf16[3,768]{1,0:T(4,128)(2,1)} %refs_0_.1, bf16[2,768]{1,0:T(2,128)(2,1)} %refs_1_.1, s32[1,768]{1,0:T(1,128)} %refs_2_.1, s32[6,24]{1,0:T(8,128)} %refs_3_.1, f32[6,24]{1,0:T(8,128)} %refs_4_.1), custom_call_target="tpu_custom_call" | custom-call | tf_op jit(solution)/shard_map/pallas_call | solution.py:345
  42.0 1.3 %copy.8 = f32[2,768]{1,0:T(2,128)} copy(f32[2,768]{1,0:T(2,128)} %shard_map.64) | data formatting | bytes 12288

commit v4 on v3

--- a/solution.py
+++ b/solution.py
@@ -214,7 +214,7 @@
         def one(b, carry):
             first, last = lax.div(b * pieces, blocks), lax.div((b + 1) * pieces, blocks)
             for i in range(-(-pieces // blocks)):
-                @pl.when((following >= 0) & (first + i < last))
+                @pl.when((following >= 0) & onward & (first + i < last))
                 def _():
                     arrive_piece(following, piece_at(first + i), onward, to)
 
@@ -254,16 +254,21 @@
     for v in range(2):
         pick = jnp.where(lax.broadcasted_iota(jnp.int32, (16, BLOCK), 0) == v, 1.0, 0.0).astype(BF16)
         v_col[v] = dot(both, pick, TN)
-    prepare(u, own_hot, False)
-    pair(u, False, from_left - 1)
-
     @pl.when(sends_left)
     def _():
         small_start(u, own_to)
         for k in range(pieces):
             moved(u, piece_at(k), own_to).start()
 
+    prepare(u, own_hot, False)
+    pair(u, False, from_left - 1)
+
     def work(j, following):
+        @pl.when((u == n - 1) & (j < half))
+        def _():
+            for k in range(pieces):
+                arrive_piece(j, piece_at(k), False, 0)
+
         hot_of(j, one_hot)
         prepare(j, one_hot, True)
         pair(j, True, following)

time: 43.5 us -> 39.2 us (0.901)
  Pallas kernels: 42 us -> 37.7 us
    pallas_call x1, Pallas kernels: 42 us -> 37.7 us  [on_device(): pl.pallas_call(functools.partial(kernel, n, tiles, blocks, exchange), out...]
where the time goes in v4:
time: 39.2 us; the launch traced here: 39 us
  Pallas kernels  37.7 us (96%)
  local copies, waits for them, and re-layouts  1.29 us (3%)
    pallas_call x1, Pallas kernels, on_device(): pl.pallas_call(functools.partial(kernel, n, tiles, blocks, exchange), out...  37.7 us
    unnamed x1, local copies, waits for them, and re-layouts  1.29 us

profile of v4, /device:TPU:0, one launch (start us, length us, event | category | flops | bytes accessed | tf_op | source)
XLA Modules:
  0.0 39.0 jit_solution(16879822816011170688)
XLA Ops:
  0.0 37.7 %shard_map.64 = f32[2,768]{1,0:T(2,128)} custom-call(bf16[8,96,256]{2,1,0:T(8,128)(2,1)} %bitcast.1, bf16[3,768]{1,0:T(4,128)(2,1)} %refs_0_.1, bf16[2,768]{1,0:T(2,128)(2,1)} %refs_1_.1, s32[1,768]{1,0:T(1,128)} %refs_2_.1, s32[6,24]{1,0:T(8,128)} %refs_3_.1, f32[6,24]{1,0:T(8,128)} %refs_4_.1), custom_call_target="tpu_custom_call" | custom-call | tf_op jit(solution)/shard_map/pallas_call | solution.py:350
  37.7 1.3 %copy.8 = f32[2,768]{1,0:T(2,128)} copy(f32[2,768]{1,0:T(2,128)} %shard_map.64) | data formatting | bytes 12288
